TPU v7x, 32 devices: a whole 2x2x4 slice. The times are simulated.
32 devices in a mesh: energy: 16 (over z, x, core), mom: 2 (over y).
Axes of the slice: x: 2, y: 2, z: 4, core: 2. Of those that a mesh axis runs over, the one named last changes fastest.
Arguments:
- sigma_in: float32 [64, 2, 2, 256, 256], P('energy', 'mom'), may hold values from -0.1875 to 0.1875
- hamiltonian: float32 [2, 2, 256, 256], P('mom'), may hold values from -0.375 to 0.375
- coupling: float32 [2, 256, 256], P('mom'), may hold values from -0.1875 to 0.1875
- energies: float32 [64], replicated, may hold values from 1.4 to 2, as said below
- counts: int32 [64], replicated, may hold values from 2 to 4, as said below
- strengths: float32 [16], replicated, may hold values from 0.05625 to 0.1875
- offsets: int32 [16], replicated, may hold values from 0 to 1
Outputs:
- sigma_next: float32 [64, 2, 2, 256, 256], P('energy', 'mom')
Inputs may be any that keep to these rules, and one draw needn't show every extreme that they name: `energies`: increasing along the grid. `counts`: each point needs either 2 or 4 sweeps, and some point needs 4.
All inputs are finite; a program needn't handle non-finite values.
Results may differ from a plain program's by a relative error of at most 0.0003.
Values sent between devices are 32-bit elements; how exact they have to be, the bound alone decides.
A program may use at most 64 MiB of HBM per device.

v0:
```python
import jax
import jax.numpy as jnp
from jax import lax
from jax.sharding import PartitionSpec as P

PRECISE = lax.Precision.HIGHEST
MIX_RATE = 0.6
PHONON = 0.1
BROADENING = 0.02


def shifted(value, axis, steps):
    count = lax.axis_size(axis)
    pairs = [(source, (source + steps) % count) for source in range(count)]
    return lax.ppermute(value, axis, pairs)


def product(left_side, right_side):
    return jnp.dot(left_side, right_side, precision=PRECISE, preferred_element_type=jnp.float32)


def invert(matrix, energy, sweeps):
    identity = jnp.eye(matrix.shape[0], dtype=jnp.float32)

    def keep_going(carried):
        return carried[0] < sweeps

    def sweep(carried):
        estimate = carried[1]
        return (carried[0] + 1, 2.0 * estimate - product(estimate, product(matrix, estimate)))

    return lax.while_loop(keep_going, sweep, (jnp.int32(0), identity / energy))[1]


def solve_point(ham_block, coupling_block, sigma_pair, energy, sweeps):
    identity = jnp.eye(ham_block.shape[1], dtype=jnp.float32)
    left_matrix = energy * identity - ham_block[0] - sigma_pair[0]
    left_inverse = invert(left_matrix, energy, sweeps)
    inverse_coupled = product(left_inverse, coupling_block)
    coupled_inverse = product(coupling_block.T, left_inverse)
    right_matrix = (
        energy * identity
        - ham_block[1]
        - sigma_pair[1]
        - product(coupling_block.T, inverse_coupled)
    )
    right_green = invert(right_matrix, energy, sweeps)
    left_green = left_inverse + product(product(inverse_coupled, right_green), coupled_inverse)
    return jnp.stack([left_green, right_green])


def lorentz(offset):
    scaled = offset / BROADENING
    return 1.0 / (1.0 + scaled * scaled)


def build_kernel(row_energy, column_energy):
    spacing = row_energy[:, None] - column_energy[None, :]
    kernel = lorentz(spacing - PHONON) + lorentz(spacing + PHONON)
    return kernel / jnp.sum(kernel, axis=1, keepdims=True)


def body(sigma_in, hamiltonian, coupling, energies, counts, strengths, offsets):
    points = sigma_in.shape[0]
    order = sigma_in.shape[3]
    ranks = lax.axis_size("energy")
    moments = lax.axis_size("mom")
    my_rank = lax.axis_index("energy")
    own_energy = lax.dynamic_slice_in_dim(energies, my_rank * points, points)
    own_count = lax.dynamic_slice_in_dim(counts, my_rank * points, points)
    blocks = sigma_in[:, 0]

    def solve_held(held_point):
        return solve_point(hamiltonian[0], coupling[0], held_point[0], held_point[1], held_point[2])

    green_blocks = lax.map(solve_held, (blocks, own_energy, own_count))
    shift_index = jnp.arange(moments, dtype=jnp.int32)
    weights = jnp.sum(
        strengths[:, None] * (offsets[:, None] == shift_index[None, :]).astype(jnp.float32), axis=0
    )
    kernel = build_kernel(energies, energies)
    piece_width = 2 * order * order // ranks
    spread = green_blocks.reshape(points, ranks, moments, piece_width // moments)
    column = lax.all_to_all(spread, "energy", split_axis=1, concat_axis=0, tiled=True)[:, 0]
    rows_all = column.shape[0]
    flat_column = column.reshape(rows_all, -1)
    mixed_sum = weights[0] * flat_column
    for offset_step in range(1, moments):
        mixed_sum = mixed_sum + weights[offset_step] * shifted(flat_column, "mom", offset_step)
    sigma_part = product(kernel, mixed_sum).reshape(column.shape)
    result = lax.all_to_all(sigma_part[:, None], "energy", split_axis=0, concat_axis=1, tiled=True)
    sigma_new = result.reshape(sigma_in.shape)
    return (1.0 - MIX_RATE) * sigma_in + MIX_RATE * sigma_new


def solution(mesh):
    placed = (
        P("energy", "mom", None, None, None),
        P("mom", None, None, None),
        P("mom", None, None),
        P(),
        P(),
        P(),
        P(),
    )
    return jax.shard_map(
        body,
        mesh=mesh,
        in_specs=placed,
        out_specs=P("energy", "mom", None, None, None),
        check_vma=False,
    )
```

profile of v0, /device:TPU:1, one launch (start us, length us, event | category | flops | bytes accessed | tf_op | source)
XLA Modules:
  0.0 263.6 jit_solution(9605364366974160668)
XLA Ops:
  0.0 0.7 dynamic_slice.18
  0.7 0.7 dynamic_slice.19
  1.5 3.0 %copy.36 = f32[4,1,2,256,256]{3,4,2,0,1:T(8,128)} copy(f32[4,1,2,256,256]{4,3,2,1,0:T(8,128)} %param.13) | data formatting | bytes 4194304 | tf_op args[0]
  4.7 73.6 %while.32 = (s32[]{:T(128)}, f32[4,2,256,256]{3,2,1,0:T(8,128)}, f32[4]{0:T(128)S(1)}, s32[4]{0:T(128)S(1)}, f32[1,2,256,256]{2,3,1,0:T(8,128)S(1)}, /*index=5*/...) while((s32[]{:T(128)}, f32[4,2,256,256]{3,2,1,0:T(8,128)}, ...), condition=%wide.region_7.8_spmd, body=%wide.region_2.7_spmd.sunk | while | flops 1813118976 | bytes 13632415 | solution.py:76
  4.7 0.7 dynamic_slice.22
  5.4 1.7 fusion.97
  8.5 3.8 %while.33 = (s32[]{:T(128)}, f32[256,256]{0,1:T(8,128)S(1)}, s32[]{:T(128)}, f32[256,256]{1,0:T(8,128)S(1)}, s32[]{:T(128)}) while((s32[]{:T(128)}, f32[256,256]{0,1:T(8,128)S(1)}, s32[]{:T(128)}, f32[256,256]{1,0:T(8,128)S(1)}, s32[]{:T(128)}) %tuple.63), condition=%wide.region_4.4_spmd, body=%wide.region_3.3_spmd.sunk | while | flops 402784256 | bytes 2097213 | solution.py:32
  9.5 0.6 fusion.109
  11.2 0.6 fusion.109
  12.3 0.6 fusion.98
  12.9 2.2 fusion.99
  15.3 3.8 %while.34 = (s32[]{:T(128)}, f32[256,256]{0,1:T(8,128)S(1)}, s32[]{:T(128)}, f32[256,256]{1,0:T(8,128)S(1)}, s32[]{:T(128)}) while((s32[]{:T(128)}, f32[256,256]{0,1:T(8,128)S(1)}, s32[]{:T(128)}, f32[256,256]{1,0:T(8,128)S(1)}, s32[]{:T(128)}) %tuple.66), condition=%wide.region_6.6_spmd, body=%wide.region_5.5_spmd.sunk | while | flops 402784256 | bytes 2097213 | solution.py:32
  16.3 0.6 fusion.115
  18.0 0.6 fusion.115
  20.6 0.8 fusion.103
  21.5 0.6 dynamic_slice.22
  22.1 1.7 fusion.97
  25.3 3.8 %while.33 = (s32[]{:T(128)}, f32[256,256]{0,1:T(8,128)S(1)}, s32[]{:T(128)}, f32[256,256]{1,0:T(8,128)S(1)}, s32[]{:T(128)}) while((s32[]{:T(128)}, f32[256,256]{0,1:T(8,128)S(1)}, s32[]{:T(128)}, f32[256,256]{1,0:T(8,128)S(1)}, s32[]{:T(128)}) %tuple.63), condition=%wide.region_4.4_spmd, body=%wide.region_3.3_spmd.sunk | while | flops 402784256 | bytes 2097213 | solution.py:32
  26.3 0.6 fusion.109
  27.9 0.6 fusion.109
  29.1 0.6 fusion.98
  29.7 2.2 fusion.99
  32.1 3.8 %while.34 = (s32[]{:T(128)}, f32[256,256]{0,1:T(8,128)S(1)}, s32[]{:T(128)}, f32[256,256]{1,0:T(8,128)S(1)}, s32[]{:T(128)}) while((s32[]{:T(128)}, f32[256,256]{0,1:T(8,128)S(1)}, s32[]{:T(128)}, f32[256,256]{1,0:T(8,128)S(1)}, s32[]{:T(128)}) %tuple.66), condition=%wide.region_6.6_spmd, body=%wide.region_5.5_spmd.sunk | while | flops 402784256 | bytes 2097213 | solution.py:32
  33.1 0.6 fusion.115
  34.7 0.6 fusion.115
  37.4 0.8 fusion.103
  38.2 0.6 dynamic_slice.22
  38.9 1.7 fusion.97
  42.1 7.1 %while.33 = (s32[]{:T(128)}, f32[256,256]{0,1:T(8,128)S(1)}, s32[]{:T(128)}, f32[256,256]{1,0:T(8,128)S(1)}, s32[]{:T(128)}) while((s32[]{:T(128)}, f32[256,256]{0,1:T(8,128)S(1)}, s32[]{:T(128)}, f32[256,256]{1,0:T(8,128)S(1)}, s32[]{:T(128)}) %tuple.63), condition=%wide.region_4.4_spmd, body=%wide.region_3.3_spmd.sunk | while | flops 402784256 | bytes 2097213 | solution.py:32
  43.1 0.6 fusion.109
  44.7 0.6 fusion.109
  46.3 0.6 fusion.109
  48.0 0.6 fusion.109
  49.1 0.6 fusion.98
  49.7 2.2 fusion.99
  52.1 7.1 %while.34 = (s32[]{:T(128)}, f32[256,256]{0,1:T(8,128)S(1)}, s32[]{:T(128)}, f32[256,256]{1,0:T(8,128)S(1)}, s32[]{:T(128)}) while((s32[]{:T(128)}, f32[256,256]{0,1:T(8,128)S(1)}, s32[]{:T(128)}, f32[256,256]{1,0:T(8,128)S(1)}, s32[]{:T(128)}) %tuple.66), condition=%wide.region_6.6_spmd, body=%wide.region_5.5_spmd.sunk | while | flops 402784256 | bytes 2097213 | solution.py:32
  53.1 0.6 fusion.115
  54.8 0.6 fusion.115
  56.4 0.6 fusion.115
  58.0 0.6 fusion.115
  60.7 0.8 fusion.103
  61.5 0.6 dynamic_slice.22
  62.2 1.7 fusion.97
  65.3 3.8 %while.33 = (s32[]{:T(128)}, f32[256,256]{0,1:T(8,128)S(1)}, s32[]{:T(128)}, f32[256,256]{1,0:T(8,128)S(1)}, s32[]{:T(128)}) while((s32[]{:T(128)}, f32[256,256]{0,1:T(8,128)S(1)}, s32[]{:T(128)}, f32[256,256]{1,0:T(8,128)S(1)}, s32[]{:T(128)}) %tuple.63), condition=%wide.region_4.4_spmd, body=%wide.region_3.3_spmd.sunk | while | flops 402784256 | bytes 2097213 | solution.py:32
  66.4 0.6 fusion.109
  68.0 0.6 fusion.109
  69.2 0.6 fusion.98
  69.8 2.2 fusion.99
  72.1 3.8 %while.34 = (s32[]{:T(128)}, f32[256,256]{0,1:T(8,128)S(1)}, s32[]{:T(128)}, f32[256,256]{1,0:T(8,128)S(1)}, s32[]{:T(128)}) while((s32[]{:T(128)}, f32[256,256]{0,1:T(8,128)S(1)}, s32[]{:T(128)}, f32[256,256]{1,0:T(8,128)S(1)}, s32[]{:T(128)}) %tuple.66), condition=%wide.region_6.6_spmd, body=%wide.region_5.5_spmd.sunk | while | flops 402784256 | bytes 2097213 | solution.py:32
  73.2 0.6 fusion.115
  74.8 0.6 fusion.115
  77.5 0.8 fusion.103
  78.3 2.6 reshape.35
  81.2 64.2 %all_to_all.24 = f32[4,16,2,4096]{3,2,0,1:T(2,128)S(1)} all-to-all(f32[4,16,2,4096]{3,2,0,1:T(2,128)S(1)} %copy.38), channel_id=1, replica_groups=mesh['energy'=16,'mom'=2] {'energy'}, dimensions={1} | all-to-all | bytes 4194304 | tf_op jit(solution)/shard_map/all_to_all | solution.py:84
  145.4 1.2 copy.41
  146.6 1.3 collective-permute-start
  148.8 45.5 %collective-permute-done = f32[64,8192]{1,0:T(8,128)S(1)} collective-permute-done((f32[64,8192]{1,0:T(8,128)S(1)}, f32[64,8192]{1,0:T(8,128)S(1)}, u32[]{:S(2)}, u32[]{:S(2)}) %collective-permute-start) | collective-permute-done | bytes 2097184 | tf_op jit(solution)/shard_map/ppermute | solution.py:15
  194.3 3.1 %fusion.13 = f32[64,8192]{1,0:T(8,128)S(1)} fusion(f32[64,8192]{1,0:T(8,128)S(1)} %collective-permute-done, f32[64,8192]{1,0:T(8,128)S(1)} %bitcast.135, f32[]{:T(128)} %bitcast.17, f32[]{:T(128)} %bitcast.13, f32[64]{0:T(128)S(1)} %fusion.31, f32[64]{0:T(128)S(1)} %copy-done.3), kind=kOutput, calls=%fused_computation.23 | convolution fusion | flops 404279296 | bytes 6291976 | tf_op jit(solution)/shard_map/dot_general | solution.py:19
  197.5 2.8 %broadcast_in_dim_reshape.3 = f32[64,1,2,4096]{3,2,0,1:T(2,128)} reshape(f32[64,8192]{1,0:T(8,128)S(1)} %fusion.13) | data formatting | bytes 4194304 | tf_op jit(solution)/shard_map/broadcast_in_dim;reshape | solution.py:91
  200.3 52.6 %all_to_all.25 = f32[64,1,2,4096]{3,2,1,0:T(2,128)S(1)} all-to-all(f32[64,1,2,4096]{3,2,1,0:T(2,128)} %bitcast.137), channel_id=1, replica_groups=mesh['energy'=16,'mom'=2] {'energy'}, dimensions={0} | all-to-all | bytes 4194304 | tf_op jit(solution)/shard_map/all_to_all | solution.py:91
  252.8 1.9 broadcast_multiply_fusion
  254.8 1.5 copy.40
  256.2 4.2 %mul.86 = f32[4,1,2,256,256]{4,3,2,1,0:T(8,128)} reshape(f32[4,16,1,2,4096]{4,3,1,0,2:T(2,128)} %copy.40) | data formatting | bytes 4194304 | tf_op jit(solution)/shard_map/mul | solution.py:93
  260.5 3.2 %multiply_add_fusion = f32[4,1,2,256,256]{4,3,2,1,0:T(8,128)} fusion(f32[4,1,2,256,256]{4,3,2,1,0:T(8,128)} %mul.86, f32[4,1,2,256,256]{4,3,2,1,0:T(8,128)S(1)} %copy-done.1), kind=kLoop, calls=%fused_computation.27 | loop fusion | flops 1048576 | bytes 6291456 | tf_op jit(solution)/shard_map/add | solution.py:93
  (98 shorter events, 19.3 us)
Async XLA Ops:
  1.5 3.0 %copy-start.2 = (f32[1,2,256,256]{3,2,1,0:T(8,128)S(1)}, f32[1,2,256,256]{3,2,1,0:T(8,128)}, u32[]{:S(2)}) copy-start(f32[1,2,256,256]{3,2,1,0:T(8,128)} %param.14) | copy-start | bytes 1572868
  1.5 3.2 %copy-start = (f32[1,256,256]{2,1,0:T(8,128)S(1)}, f32[1,256,256]{2,1,0:T(8,128)}, u32[]{:S(2)}) copy-start(f32[1,256,256]{2,1,0:T(8,128)} %param.15) | copy-start | bytes 786436
  145.4 2.5 copy-start.4
  145.4 2.5 copy-start.5
  145.4 3.2 %copy-start.3 = (f32[64]{0:T(128)S(1)}, f32[64]{0:T(128)}, u32[]{:S(2)}) copy-start(f32[64]{0:T(128)} %param.16) | copy-start | bytes 772
  146.6 47.7 %collective-permute-start = (f32[64,8192]{1,0:T(8,128)S(1)}, f32[64,8192]{1,0:T(8,128)S(1)}, u32[]{:S(2)}, u32[]{:S(2)}) collective-permute-start(f32[64,8192]{1,0:T(8,128)S(1)} %bitcast.134), channel_id=1, source_target_pairs={{0,1},{1,0},{2,3},{3,2},{4,5},{5,4},{6,7},{7,6},{8,9},{9,8},{10,11... | collective-permute-start | bytes 6291464 | tf_op jit(solution)/shard_map/ppermute | solution.py:15
  256.2 4.2 %copy-start.1 = (f32[4,1,2,256,256]{4,3,2,1,0:T(8,128)S(1)}, f32[4,1,2,256,256]{4,3,2,1,0:T(8,128)}, u32[]{:S(2)}) copy-start(f32[4,1,2,256,256]{4,3,2,1,0:T(8,128)} %param.13) | copy-start | bytes 6291460
where the time goes:
time: 265 us; the launch traced here: 264 us
  blocking collectives  117 us (44%)
  waiting for transfers between devices  45.5 us (17%)
  matrix products  39.5 us (15%)
  local copies, waits for them, and re-layouts  25.2 us (10%)
  loops' own time  19.8 us (7%)
  other arithmetic  15.5 us (6%)
    all_to_all x1, blocking collectives, body(): lax.all_to_all(spread, 'energy', split_axis=1, concat_axis=0, tiled=True)  64.2 us
    all_to_all x1, blocking collectives, body(): lax.all_to_all(sigma_part[:, None], 'energy', split_axis=0, concat_axis=1...  52.6 us
    ppermute x1, waiting for transfers between devices, shifted(): return lax.ppermute(value, axis, pairs)  45.5 us
    dot_general x61, matrix products, product(): jnp.dot(left_side, right_side, precision=PRECISE, preferred_element_type=...  39.5 us
    another operation x8, loops' own time, invert(): lax.while_loop(keep_going, sweep, (jnp.int32(0), identity / energy))[1]  16.5 us
    sub x4, other arithmetic, solve_point(): left_matrix = energy * identity - ham_block[0] - sigma_pair[0]  6.66 us
    mul x2, local copies, waits for them, and re-layouts, body(): return (1.0 - MIX_RATE) * sigma_in + MIX_RATE * sigma_new  5.67 us
  transfers between devices with their start and end apart: 1, of which 1 were waited for; matrix products, arithmetic and copies ran while one was open for 0% of the time, Pallas kernels for 0%

commit v1 on v0

--- a/solution.py
+++ b/solution.py
@@ -81,7 +81,20 @@
     kernel = build_kernel(energies, energies)
     piece_width = 2 * order * order // ranks
     spread = green_blocks.reshape(points, ranks, moments, piece_width // moments)
-    column = lax.all_to_all(spread, "energy", split_axis=1, concat_axis=0, tiled=True)[:, 0]
+
+    def produce_shelves(in_array, axis_tag):
+        w2 = jnp.concatenate(
+            lax.all_to_all(
+                jnp.stack(jnp.split(in_array, lax.axis_size(axis_tag), 1), axis=0),
+                axis_tag,
+                concat_axis=0,
+                split_axis=0,
+            ),
+            axis=0,
+        )
+        return w2
+
+    column = produce_shelves(spread, "energy")[:, 0]
     rows_all = column.shape[0]
     flat_column = column.reshape(rows_all, -1)
     mixed_sum = weights[0] * flat_column

time: 265 us -> 265 us (level)
  no operation moved by 1% of the time
where the time goes in v1:
time: 265 us; the launch traced here: 264 us
  blocking collectives  117 us (44%)
  waiting for transfers between devices  45.5 us (17%)
  matrix products  39.5 us (15%)
  local copies, waits for them, and re-layouts  25.3 us (10%)
  loops' own time  19.8 us (7%)
  other arithmetic  15.5 us (6%)
    all_to_all x1, blocking collectives, produce_shelves(): lax.all_to_all(jnp.stack(jnp.split(in_array, lax.axis_size(axis_tag), 1),...  64.2 us
    all_to_all x1, blocking collectives, body(): lax.all_to_all(sigma_part[:, None], 'energy', split_axis=0, concat_axis=1...  52.6 us
    ppermute x1, waiting for transfers between devices, shifted(): return lax.ppermute(value, axis, pairs)  45.5 us
    dot_general x61, matrix products, product(): jnp.dot(left_side, right_side, precision=PRECISE, preferred_element_type=...  39.5 us
    another operation x8, loops' own time, invert(): lax.while_loop(keep_going, sweep, (jnp.int32(0), identity / energy))[1]  16.5 us
    sub x4, other arithmetic, solve_point(): left_matrix = energy * identity - ham_block[0] - sigma_pair[0]  6.66 us
    mul x2, local copies, waits for them, and re-layouts, body(): return (1.0 - MIX_RATE) * sigma_in + MIX_RATE * sigma_new  5.67 us
  transfers between devices with their start and end apart: 1, of which 1 were waited for; matrix products, arithmetic and copies ran while one was open for 0% of the time, Pallas kernels for 0%

profile of v1, /device:TPU:1, one launch (start us, length us, event | category | flops | bytes accessed | tf_op | source)
XLA Modules:
  0.0 263.8 jit_solution(6706498523941754992)
XLA Ops:
  0.0 0.7 dynamic_slice.18
  0.7 0.7 dynamic_slice.19
  1.5 3.0 %copy.57 = f32[4,1,2,256,256]{3,4,2,0,1:T(8,128)} copy(f32[4,1,2,256,256]{4,3,2,1,0:T(8,128)} %param.13) | data formatting | bytes 4194304 | tf_op args[0]
  4.7 73.6 %while.32 = (s32[]{:T(128)}, f32[4,2,256,256]{3,2,1,0:T(8,128)}, f32[4]{0:T(128)S(1)}, s32[4]{0:T(128)S(1)}, f32[1,2,256,256]{2,3,1,0:T(8,128)S(1)}, /*index=5*/...) while((s32[]{:T(128)}, f32[4,2,256,256]{3,2,1,0:T(8,128)}, ...), condition=%wide.region_7.8_spmd, body=%wide.region_2.7_spmd.sunk | while | flops 1813118976 | bytes 13632415 | solution.py:76
  4.7 0.7 dynamic_slice.22
  5.4 1.7 fusion.113
  8.5 3.8 %while.33 = (s32[]{:T(128)}, f32[256,256]{0,1:T(8,128)S(1)}, s32[]{:T(128)}, f32[256,256]{1,0:T(8,128)S(1)}, s32[]{:T(128)}) while((s32[]{:T(128)}, f32[256,256]{0,1:T(8,128)S(1)}, s32[]{:T(128)}, f32[256,256]{1,0:T(8,128)S(1)}, s32[]{:T(128)}) %tuple.60), condition=%wide.region_4.4_spmd, body=%wide.region_3.3_spmd.sunk | while | flops 402784256 | bytes 2097213 | solution.py:32
  9.5 0.6 fusion.125
  11.2 0.6 fusion.125
  12.3 0.6 fusion.114
  12.9 2.2 fusion.115
  15.3 3.8 %while.34 = (s32[]{:T(128)}, f32[256,256]{0,1:T(8,128)S(1)}, s32[]{:T(128)}, f32[256,256]{1,0:T(8,128)S(1)}, s32[]{:T(128)}) while((s32[]{:T(128)}, f32[256,256]{0,1:T(8,128)S(1)}, s32[]{:T(128)}, f32[256,256]{1,0:T(8,128)S(1)}, s32[]{:T(128)}) %tuple.63), condition=%wide.region_6.6_spmd, body=%wide.region_5.5_spmd.sunk | while | flops 402784256 | bytes 2097213 | solution.py:32
  16.3 0.6 fusion.131
  18.0 0.6 fusion.131
  20.6 0.8 fusion.119
  21.5 0.6 dynamic_slice.22
  22.1 1.7 fusion.113
  25.3 3.8 %while.33 = (s32[]{:T(128)}, f32[256,256]{0,1:T(8,128)S(1)}, s32[]{:T(128)}, f32[256,256]{1,0:T(8,128)S(1)}, s32[]{:T(128)}) while((s32[]{:T(128)}, f32[256,256]{0,1:T(8,128)S(1)}, s32[]{:T(128)}, f32[256,256]{1,0:T(8,128)S(1)}, s32[]{:T(128)}) %tuple.60), condition=%wide.region_4.4_spmd, body=%wide.region_3.3_spmd.sunk | while | flops 402784256 | bytes 2097213 | solution.py:32
  26.3 0.6 fusion.125
  27.9 0.6 fusion.125
  29.1 0.6 fusion.114
  29.7 2.2 fusion.115
  32.1 3.8 %while.34 = (s32[]{:T(128)}, f32[256,256]{0,1:T(8,128)S(1)}, s32[]{:T(128)}, f32[256,256]{1,0:T(8,128)S(1)}, s32[]{:T(128)}) while((s32[]{:T(128)}, f32[256,256]{0,1:T(8,128)S(1)}, s32[]{:T(128)}, f32[256,256]{1,0:T(8,128)S(1)}, s32[]{:T(128)}) %tuple.63), condition=%wide.region_6.6_spmd, body=%wide.region_5.5_spmd.sunk | while | flops 402784256 | bytes 2097213 | solution.py:32
  33.1 0.6 fusion.131
  34.7 0.6 fusion.131
  37.4 0.8 fusion.119
  38.2 0.6 dynamic_slice.22
  38.9 1.7 fusion.113
  42.1 7.1 %while.33 = (s32[]{:T(128)}, f32[256,256]{0,1:T(8,128)S(1)}, s32[]{:T(128)}, f32[256,256]{1,0:T(8,128)S(1)}, s32[]{:T(128)}) while((s32[]{:T(128)}, f32[256,256]{0,1:T(8,128)S(1)}, s32[]{:T(128)}, f32[256,256]{1,0:T(8,128)S(1)}, s32[]{:T(128)}) %tuple.60), condition=%wide.region_4.4_spmd, body=%wide.region_3.3_spmd.sunk | while | flops 402784256 | bytes 2097213 | solution.py:32
  43.1 0.6 fusion.125
  44.7 0.6 fusion.125
  46.3 0.6 fusion.125
  48.0 0.6 fusion.125
  49.1 0.6 fusion.114
  49.7 2.2 fusion.115
  52.1 7.1 %while.34 = (s32[]{:T(128)}, f32[256,256]{0,1:T(8,128)S(1)}, s32[]{:T(128)}, f32[256,256]{1,0:T(8,128)S(1)}, s32[]{:T(128)}) while((s32[]{:T(128)}, f32[256,256]{0,1:T(8,128)S(1)}, s32[]{:T(128)}, f32[256,256]{1,0:T(8,128)S(1)}, s32[]{:T(128)}) %tuple.63), condition=%wide.region_6.6_spmd, body=%wide.region_5.5_spmd.sunk | while | flops 402784256 | bytes 2097213 | solution.py:32
  53.1 0.6 fusion.131
  54.8 0.6 fusion.131
  56.4 0.6 fusion.131
  58.0 0.6 fusion.131
  60.7 0.8 fusion.119
  61.5 0.6 dynamic_slice.22
  62.2 1.7 fusion.113
  65.3 3.8 %while.33 = (s32[]{:T(128)}, f32[256,256]{0,1:T(8,128)S(1)}, s32[]{:T(128)}, f32[256,256]{1,0:T(8,128)S(1)}, s32[]{:T(128)}) while((s32[]{:T(128)}, f32[256,256]{0,1:T(8,128)S(1)}, s32[]{:T(128)}, f32[256,256]{1,0:T(8,128)S(1)}, s32[]{:T(128)}) %tuple.60), condition=%wide.region_4.4_spmd, body=%wide.region_3.3_spmd.sunk | while | flops 402784256 | bytes 2097213 | solution.py:32
  66.4 0.6 fusion.125
  68.0 0.6 fusion.125
  69.2 0.6 fusion.114
  69.8 2.2 fusion.115
  72.1 3.8 %while.34 = (s32[]{:T(128)}, f32[256,256]{0,1:T(8,128)S(1)}, s32[]{:T(128)}, f32[256,256]{1,0:T(8,128)S(1)}, s32[]{:T(128)}) while((s32[]{:T(128)}, f32[256,256]{0,1:T(8,128)S(1)}, s32[]{:T(128)}, f32[256,256]{1,0:T(8,128)S(1)}, s32[]{:T(128)}) %tuple.63), condition=%wide.region_6.6_spmd, body=%wide.region_5.5_spmd.sunk | while | flops 402784256 | bytes 2097213 | solution.py:32
  73.2 0.6 fusion.131
  74.8 0.6 fusion.131
  77.5 0.8 fusion.119
  78.3 2.6 reshape.34
  81.4 64.2 %all_to_all.14 = f32[16,4,1,2,4096]{4,3,1,2,0:T(2,128)S(1)} all-to-all(f32[16,4,1,2,4096]{4,3,1,2,0:T(2,128)S(1)} %fusion.19), channel_id=1, replica_groups=mesh['energy'=16,'mom'=2] {'energy'}, dimensions={0} | all-to-all | bytes 4194304 | tf_op jit(solution)/shard_map/all_to_all | solution.py:87
  145.6 1.2 copy.91
  146.8 1.3 collective-permute-start
  149.0 45.5 %collective-permute-done = f32[64,8192]{1,0:T(8,128)S(1)} collective-permute-done((f32[64,8192]{1,0:T(8,128)S(1)}, f32[64,8192]{1,0:T(8,128)S(1)}, u32[]{:S(2)}, u32[]{:S(2)}) %collective-permute-start) | collective-permute-done | bytes 2097184 | tf_op jit(solution)/shard_map/ppermute | solution.py:15
  194.5 3.2 %fusion.13 = f32[64,8192]{1,0:T(8,128)S(1)} fusion(f32[64,8192]{1,0:T(8,128)S(1)} %collective-permute-done, f32[64,8192]{1,0:T(8,128)S(1)} %bitcast.226, f32[]{:T(128)} %bitcast.31, f32[]{:T(128)} %bitcast.13, f32[64]{0:T(128)S(1)} %fusion.47, f32[64]{0:T(128)S(1)} %copy-done.3), kind=kOutput, calls=%fused_computation.23 | convolution fusion | flops 404279296 | bytes 6291976 | tf_op jit(solution)/shard_map/dot_general | solution.py:19
  197.7 2.8 %broadcast_in_dim_reshape.3 = f32[64,1,2,4096]{3,2,0,1:T(2,128)} reshape(f32[64,8192]{1,0:T(8,128)S(1)} %fusion.13) | data formatting | bytes 4194304 | tf_op jit(solution)/shard_map/broadcast_in_dim;reshape | solution.py:104
  200.5 52.6 %all_to_all.15 = f32[64,1,2,4096]{3,2,1,0:T(2,128)S(1)} all-to-all(f32[64,1,2,4096]{3,2,1,0:T(2,128)} %bitcast.228), channel_id=1, replica_groups=mesh['energy'=16,'mom'=2] {'energy'}, dimensions={0} | all-to-all | bytes 4194304 | tf_op jit(solution)/shard_map/all_to_all | solution.py:104
  253.0 1.9 broadcast_multiply_fusion
  255.0 1.5 copy.75
  256.4 4.2 %mul.86 = f32[4,1,2,256,256]{4,3,2,1,0:T(8,128)} reshape(f32[4,16,1,2,4096]{4,3,1,0,2:T(2,128)} %copy.75) | data formatting | bytes 4194304 | tf_op jit(solution)/shard_map/mul | solution.py:106
  260.6 3.2 %multiply_add_fusion = f32[4,1,2,256,256]{4,3,2,1,0:T(8,128)} fusion(f32[4,1,2,256,256]{4,3,2,1,0:T(8,128)} %mul.86, f32[4,1,2,256,256]{4,3,2,1,0:T(8,128)S(1)} %copy-done.1), kind=kLoop, calls=%fused_computation.27 | loop fusion | flops 1048576 | bytes 6291456 | tf_op jit(solution)/shard_map/add | solution.py:106
  (113 shorter events, 19.4 us)
Async XLA Ops:
  1.5 3.0 %copy-start.2 = (f32[1,2,256,256]{3,2,1,0:T(8,128)S(1)}, f32[1,2,256,256]{3,2,1,0:T(8,128)}, u32[]{:S(2)}) copy-start(f32[1,2,256,256]{3,2,1,0:T(8,128)} %param.14) | copy-start | bytes 1572868
  1.5 3.2 %copy-start = (f32[1,256,256]{2,1,0:T(8,128)S(1)}, f32[1,256,256]{2,1,0:T(8,128)}, u32[]{:S(2)}) copy-start(f32[1,256,256]{2,1,0:T(8,128)} %param.15) | copy-start | bytes 786436
  145.6 2.5 copy-start.4
  145.6 2.5 copy-start.5
  145.6 3.2 %copy-start.3 = (f32[64]{0:T(128)S(1)}, f32[64]{0:T(128)}, u32[]{:S(2)}) copy-start(f32[64]{0:T(128)} %param.16) | copy-start | bytes 772
  146.8 47.7 %collective-permute-start = (f32[64,8192]{1,0:T(8,128)S(1)}, f32[64,8192]{1,0:T(8,128)S(1)}, u32[]{:S(2)}, u32[]{:S(2)}) collective-permute-start(f32[64,8192]{1,0:T(8,128)S(1)} %bitcast.225), channel_id=1, source_target_pairs={{0,1},{1,0},{2,3},{3,2},{4,5},{5,4},{6,7},{7,6},{8,9},{9,8},{10,11... | collective-permute-start | bytes 6291464 | tf_op jit(solution)/shard_map/ppermute | solution.py:15
  256.4 4.2 %copy-start.1 = (f32[4,1,2,256,256]{4,3,2,1,0:T(8,128)S(1)}, f32[4,1,2,256,256]{4,3,2,1,0:T(8,128)}, u32[]{:S(2)}) copy-start(f32[4,1,2,256,256]{4,3,2,1,0:T(8,128)} %param.13) | copy-start | bytes 6291460
